TPU v7x, 32 devices: a whole 2x2x4 slice. The times are simulated.
32 devices in a mesh: gx: 4 (over z), gy: 8 (over y, x, core).
Axes of the slice: x: 2, y: 2, z: 4, core: 2. Of those that a mesh axis runs over, the one named last changes fastest.
Arguments:
- conductivity: bfloat16 [2, 1024, 4096], P(None, 'gy', 'gx'), may hold values from 0.099609375 to 1.59375
Outputs:
- coarse_stencil: float32 [9, 8, 64, 2048], P(None, 'gy', 'gx')
All inputs are finite; a program needn't handle non-finite values.
Results may differ from a plain program's by a relative error of at most 0.0003.
Values may be sent and summed in bfloat16 or wider, within the bound.
A program may use at most 64 MiB of HBM per device.

v0:
```python
from functools import partial
import jax
import jax.numpy as jnp
from jax import lax
from jax.sharding import PartitionSpec as P


def with_halo(cells, sides, width):
    for axis, dim in sides:
        count = lax.axis_size(axis)
        ends = count - 1
        head = lax.slice_in_dim(cells, 0, width, axis=dim)
        tail = lax.slice_in_dim(cells, cells.shape[dim] - width, cells.shape[dim], axis=dim)
        cells = jnp.concatenate(
            [
                lax.ppermute(tail, axis, [(i, (i + 1) % count) for i in range(ends)]),
                cells,
                lax.ppermute(head, axis, [((i + 1) % count, i) for i in range(ends)]),
            ],
            axis=dim,
        )
    return cells


def harmonic(first, second):
    return 2.0 * first * second / (first + second)


def prepare_window(extended, row_start, col_start, rows_all, cols_all, used_rows, used_cols):
    conduct = extended.astype(jnp.float32)
    ext_rows = conduct.shape[1]
    ext_cols = conduct.shape[2]
    row_places = jnp.arange(ext_rows, dtype=jnp.int32)
    col_places = jnp.arange(ext_cols, dtype=jnp.int32)
    row_ids = row_start - 2 + row_places
    col_ids = col_start - 2 + col_places
    row_inside = (row_ids >= 0) & (row_ids < rows_all) & (row_places < used_rows)
    col_inside = (col_ids >= 0) & (col_ids < cols_all) & (col_places < used_cols)
    inside = row_inside[:, None] & col_inside[None, :]
    safe_values = jnp.where(inside[None], conduct, 1.0)
    east_face = jnp.where(
        jnp.roll(inside, -1, 1)[None],
        harmonic(safe_values, jnp.roll(safe_values, -1, 2)),
        safe_values,
    )
    west_face = jnp.where(
        jnp.roll(inside, 1, 1)[None],
        harmonic(safe_values, jnp.roll(safe_values, 1, 2)),
        safe_values,
    )
    north_face = jnp.where(
        jnp.roll(inside, -1, 0)[None],
        harmonic(safe_values, jnp.roll(safe_values, -1, 1)),
        safe_values,
    )
    south_face = jnp.where(
        jnp.roll(inside, 1, 0)[None],
        harmonic(safe_values, jnp.roll(safe_values, 1, 1)),
        safe_values,
    )
    vertical = harmonic(safe_values[0], safe_values[1])
    centre = east_face + west_face + north_face + south_face + vertical[None] + safe_values
    col_east = east_face[0] + east_face[1]
    col_west = west_face[0] + west_face[1]
    row_north = north_face[0] + north_face[1]
    row_south = south_face[0] + south_face[1]
    left_weight = col_west / (col_west + col_east)
    right_weight = col_east / (col_west + col_east)
    south_weight = row_south / (row_south + row_north)
    north_weight = row_north / (row_south + row_north)
    odd_rows = (row_ids % 2 == 1)[:, None]
    odd_cols = (col_ids % 2 == 1)[None, :]
    even_point = inside & (row_ids % 2 == 0)[:, None] & (col_ids % 2 == 0)[None, :]
    row_class = (row_ids // 2 % 3)[:, None]
    col_class = (col_ids // 2 % 3)[None, :]
    return (
        inside,
        odd_rows,
        odd_cols,
        even_point,
        row_class,
        col_class,
        east_face,
        west_face,
        north_face,
        south_face,
        vertical,
        centre,
        left_weight,
        right_weight,
        south_weight,
        north_weight,
    )


def probe_rows(prepared, local_rows, colour):
    (
        inside,
        odd_rows,
        odd_cols,
        even_point,
        row_class,
        col_class,
        east_face,
        west_face,
        north_face,
        south_face,
        vertical,
        centre,
        left_weight,
        right_weight,
        south_weight,
        north_weight,
    ) = prepared
    chosen = even_point & (row_class == colour // 3) & (col_class == colour % 3)
    probe_field = chosen.astype(jnp.float32)
    along_x = jnp.where(
        odd_cols,
        left_weight * jnp.roll(probe_field, 1, 1) + right_weight * jnp.roll(probe_field, -1, 1),
        probe_field,
    )
    fine_field = jnp.where(
        odd_rows,
        south_weight * jnp.roll(along_x, 1, 0) + north_weight * jnp.roll(along_x, -1, 0),
        along_x,
    )
    fine_field = jnp.where(inside, fine_field, 0.0)
    applied = (
        centre * fine_field
        - east_face * jnp.roll(fine_field, -1, 1)
        - west_face * jnp.roll(fine_field, 1, 1)
        - north_face * jnp.roll(fine_field, -1, 0)
        - south_face * jnp.roll(fine_field, 1, 0)
        - vertical * fine_field
    )
    folded = jnp.where(inside, applied[0] + applied[1], 0.0)
    rows_done = (
        folded + jnp.roll(south_weight * folded, -1, 0) + jnp.roll(north_weight * folded, 1, 0)
    )
    cols_done = (
        rows_done
        + jnp.roll(left_weight * rows_done, -1, 1)
        + jnp.roll(right_weight * rows_done, 1, 1)
    )
    width = cols_done.shape[1]
    kept = cols_done[2 : 2 + local_rows].reshape(local_rows // 2, 2, width)
    return kept[:, 0]


def by_offset(colours, row_first, col_first):
    count_rows = colours.shape[1]
    count_cols = colours.shape[2]
    coarse_rows = row_first + jnp.arange(count_rows, dtype=jnp.int32)
    coarse_cols = col_first + jnp.arange(count_cols, dtype=jnp.int32)
    fields = []
    for step_row in (-1, 0, 1):
        for step_col in (-1, 0, 1):
            row_group = (coarse_rows + step_row) % 3
            col_group = (coarse_cols + step_col) % 3
            selected = jnp.zeros((count_rows, count_cols), jnp.float32)
            for colour in range(9):
                chosen = (row_group == colour // 3)[:, None] & (col_group == colour % 3)[None, :]
                selected = jnp.where(chosen, colours[colour], selected)
            fields.append(selected)
    return jnp.stack(fields)


def shards(conductivity):
    local_rows = conductivity.shape[1]
    local_cols = conductivity.shape[2]
    row_start = lax.axis_index("gy") * local_rows
    col_start = lax.axis_index("gx") * local_cols
    rows_all = local_rows * lax.axis_size("gy")
    cols_all = local_cols * lax.axis_size("gx")
    extended = with_halo(conductivity, (("gx", 2), ("gy", 1)), 2)
    used_rows = local_rows + 4
    used_cols = local_cols + 4
    row_fill = -used_rows % 8
    col_fill = -used_cols % 128
    aligned = jnp.pad(extended, ((0, 0), (0, row_fill), (0, col_fill)))
    prepared = prepare_window(
        aligned, row_start, col_start, rows_all, cols_all, used_rows, used_cols
    )
    row_picked = lax.map(partial(probe_rows, prepared, local_rows), jnp.arange(9, dtype=jnp.int32))
    width = row_picked.shape[2]
    half_cols = local_cols // 2
    picker = (
        jnp.arange(width, dtype=jnp.int32)[:, None]
        == 2 + 2 * jnp.arange(half_cols, dtype=jnp.int32)[None, :]
    ).astype(jnp.float32)
    flat_rows = row_picked.reshape(9 * (local_rows // 2), width)
    colours = jnp.dot(
        flat_rows, picker, precision=lax.Precision.HIGHEST, preferred_element_type=jnp.float32
    )
    colours = colours.reshape(9, local_rows // 2, half_cols)
    stencil = by_offset(colours, row_start // 2, col_start // 2)
    moved = lax.all_to_all(stencil, "gx", split_axis=1, concat_axis=2, tiled=True)
    return moved[:, None]


def solution(mesh):
    in_specs = (P(None, "gy", "gx"),)
    out_specs = P(None, "gy", "gx", None)
    return jax.shard_map(shards, mesh=mesh, in_specs=in_specs, out_specs=out_specs, check_vma=False)
```

profile of v0, /device:TPU:4, one launch (start us, length us, event | category | flops | bytes accessed | tf_op | source)
XLA Modules:
  0.0 210.9 jit_solution(8876209915577884419)
XLA Ops:
  1.0 3.5 %collective-permute-start = (bf16[2,128,2]{2,1,0:T(8,128)(2,1)S(1)}, bf16[2,128,2]{2,1,0:T(8,128)(2,1)S(1)}, u32[]{:S(2)}, u32[]{:S(2)}) collective-permute-start(bf16[2,128,2]{2,1,0:T(8,128)(2,1)S(1)} %get-tuple-element.442), channel_id=1, source_target_pairs={{0,8},{8,16},{16,24},{1,9},{9,17},{17,25},{2,10},{10,18},{18,26},{... | collective-permute-start | bytes 3080 | tf_op jit(solution)/shard_map/ppermute | solution.py:16
  4.5 1.3 collective-permute-start.1
  7.1 3.5 %collective-permute-done.1 = bf16[2,128,2]{2,1,0:T(8,128)(2,1)S(1)} collective-permute-done((bf16[2,128,2]{2,1,0:T(8,128)(2,1)S(1)}, bf16[2,128,2]{2,1,0:T(8,128)(2,1)S(1)}, u32[]{:S(2)}, u32[]{:S(2)}) %collective-permute-start.1) | collective-permute-done | bytes 1056 | tf_op jit(solution)/shard_map/ppermute | solution.py:18
  11.3 1.9 collective-permute-start.2
  13.2 4.5 %collective-permute-start.3 = (bf16[2,2,1028]{2,1,0:T(2,128)(2,1)S(1)}, bf16[2,2,1028]{2,1,0:T(2,128)(2,1)S(1)}, u32[]{:S(2)}, u32[]{:S(2)}) collective-permute-start(bf16[2,2,1028]{2,1,0:T(2,128)(2,1)S(1)} %get-tuple-element.440), channel_id=1, source_target_pairs={{1,0},{2,1},{3,2},{4,3},{5,4},{6,5},{7,6},{9,8},{10,9},{11,10},{12... | collective-permute-start | bytes 24680 | tf_op jit(solution)/shard_map/ppermute | solution.py:18
  17.8 1.3 collective-permute-done.3
  21.1 4.2 %add_add_fusion = (f32[2,136,1152]{2,1,0:T(8,128)}, f32[2,136,1152]{2,1,0:T(8,128)S(1)}, f32[2,136,1152]{2,1,0:T(8,128)S(1)}, f32[2,136,1152]{2,1,0:T(8,128)S(1)}, f32[2,136,1152]{2,1,0:T(8,128)S(1)}) fusion(f32[136,1152]{1,0:T(8,128)S(1)} %divide_bitcast_fusion, pred[136,1152]{1,0:T(8,128)(4,1)S(1)} %broadcast_and_fusion, ...), kind=kLoop, calls=%fused_computation.66 | loop fusion | flops 13160448 | bytes 13233216 | tf_op jit(solution)/shard_map/add | solution.py:62
  27.6 121.1 %while.14 = (s32[]{:T(128)}, f32[9,64,1152]{2,1,0:T(8,128)}, s32[9]{0:T(128)S(1)}, f32[136,1152]{1,0:T(8,128)S(1)}, f32[136,1152]{1,0:T(8,128)S(1)}, /*index=5*/...) while((s32[]{:T(128)}, f32[9,64,1152]{2,1,0:T(8,128)}, ...), condition=%wide.region_1.2_spmd.clone.clone, body=%wide.region_0.1_spmd.clone.clone.sunk | while | flops 10339566 | bytes 78140304 | solution.py:184
  31.2 1.4 fusion.104
  39.1 1.3 slice_bitcast_fusion.2
  44.6 1.4 fusion.104
  58.1 1.4 fusion.104
  71.5 1.4 fusion.104
  79.4 1.3 slice_bitcast_fusion.2
  85.0 1.4 fusion.104
  92.9 1.3 slice_bitcast_fusion.2
  98.4 1.4 fusion.104
  106.3 1.3 slice_bitcast_fusion.2
  111.9 1.4 fusion.104
  125.4 1.4 fusion.104
  138.8 1.4 fusion.104
  148.7 4.3 %fusion.23 = f32[576,512]{1,0:T(8,128)S(1)} fusion(f32[576,1152]{1,0:T(8,128)} %bitcast.88, s32[512]{0:T(512)S(1)} %multiply_add_fusion), kind=kOutput, calls=%fused_computation.55 | convolution fusion | flops 4077453312 | bytes 3835904 | tf_op jit(solution)/shard_map/dot_general | solution.py:192
  155.7 52.7 %all_to_all.15 = f32[9,64,512]{2,0,1:T(8,128)S(1)} all-to-all(f32[9,64,512]{2,0,1:T(8,128)S(1)} %copy.7), channel_id=1, replica_groups=mesh['gx'=4,'gy'=8] {'gx'}, dimensions={1} | all-to-all | bytes 2359296 | tf_op jit(solution)/shard_map/all_to_all | solution.py:197
  209.1 1.8 broadcast_in_dim.97
  (433 shorter events, 96.7 us)
Async XLA Ops:
  1.0 6.1 %collective-permute-start = (bf16[2,128,2]{2,1,0:T(8,128)(2,1)S(1)}, bf16[2,128,2]{2,1,0:T(8,128)(2,1)S(1)}, u32[]{:S(2)}, u32[]{:S(2)}) collective-permute-start(bf16[2,128,2]{2,1,0:T(8,128)(2,1)S(1)} %get-tuple-element.442), channel_id=1, source_target_pairs={{0,8},{8,16},{16,24},{1,9},{9,17},{17,25},{2,10},{10,18},{18,26},{... | collective-permute-start | bytes 3080 | tf_op jit(solution)/shard_map/ppermute | solution.py:16
  4.5 6.2 %collective-permute-start.1 = (bf16[2,128,2]{2,1,0:T(8,128)(2,1)S(1)}, bf16[2,128,2]{2,1,0:T(8,128)(2,1)S(1)}, u32[]{:S(2)}, u32[]{:S(2)}) collective-permute-start(bf16[2,128,2]{2,1,0:T(8,128)(2,1)S(1)} %get-tuple-element.441), channel_id=1, source_target_pairs={{8,0},{16,8},{24,16},{9,1},{17,9},{25,17},{10,2},{18,10},{26,18},{... | collective-permute-start | bytes 3080 | tf_op jit(solution)/shard_map/ppermute | solution.py:18
  5.9 4.7 %copy-start.9 = (bf16[2,128,1024]{2,1,0:T(8,128)(2,1)S(1)}, bf16[2,128,1024]{2,1,0:T(8,128)(2,1)}, u32[]{:S(2)}) copy-start(bf16[2,128,1024]{2,1,0:T(8,128)(2,1)} %param.3) | copy-start | bytes 1572868
  11.3 6.5 %collective-permute-start.2 = (bf16[2,2,1028]{2,1,0:T(2,128)(2,1)S(1)}, bf16[2,2,1028]{2,1,0:T(2,128)(2,1)S(1)}, u32[]{:S(2)}, u32[]{:S(2)}) collective-permute-start(bf16[2,2,1028]{2,1,0:T(2,128)(2,1)S(1)} %get-tuple-element.439), channel_id=1, source_target_pairs={{0,1},{1,2},{2,3},{3,4},{4,5},{5,6},{6,7},{8,9},{9,10},{10,11},{11... | collective-permute-start | bytes 24680 | tf_op jit(solution)/shard_map/ppermute | solution.py:16
  13.2 5.9 %collective-permute-start.3 = (bf16[2,2,1028]{2,1,0:T(2,128)(2,1)S(1)}, bf16[2,2,1028]{2,1,0:T(2,128)(2,1)S(1)}, u32[]{:S(2)}, u32[]{:S(2)}) collective-permute-start(bf16[2,2,1028]{2,1,0:T(2,128)(2,1)S(1)} %get-tuple-element.440), channel_id=1, source_target_pairs={{1,0},{2,1},{3,2},{4,3},{5,4},{6,5},{7,6},{9,8},{10,9},{11,10},{12... | collective-permute-start | bytes 24680 | tf_op jit(solution)/shard_map/ppermute | solution.py:18
  25.3 2.3 %copy-start.6 = (f32[2,136,1152]{2,1,0:T(8,128)}, f32[2,136,1152]{2,1,0:T(8,128)S(1)}, u32[]{:S(2)}) copy-start(f32[2,136,1152]{2,1,0:T(8,128)S(1)} %get-tuple-element.647) | copy-start | bytes 3760132
  33.4 2.2 %copy-start.1 = (f32[2,136,1152]{2,1,0:T(8,128)S(1)}, f32[2,136,1152]{2,1,0:T(8,128)}, u32[]{:S(2)}) copy-start(f32[2,136,1152]{2,1,0:T(8,128)} %get-tuple-element.698) | copy-start | bytes 3760132 | tf_op jit(solution)/shard_map/while
  33.4 2.5 %copy-start.3 = (f32[2,136,1152]{2,1,0:T(8,128)S(1)}, f32[2,136,1152]{2,1,0:T(8,128)}, u32[]{:S(2)}) copy-start(f32[2,136,1152]{2,1,0:T(8,128)} %get-tuple-element.699) | copy-start | bytes 3760132 | tf_op jit(solution)/shard_map/while
  46.8 2.2 %copy-start.1 = (f32[2,136,1152]{2,1,0:T(8,128)S(1)}, f32[2,136,1152]{2,1,0:T(8,128)}, u32[]{:S(2)}) copy-start(f32[2,136,1152]{2,1,0:T(8,128)} %get-tuple-element.698) | copy-start | bytes 3760132 | tf_op jit(solution)/shard_map/while
  46.9 2.5 %copy-start.3 = (f32[2,136,1152]{2,1,0:T(8,128)S(1)}, f32[2,136,1152]{2,1,0:T(8,128)}, u32[]{:S(2)}) copy-start(f32[2,136,1152]{2,1,0:T(8,128)} %get-tuple-element.699) | copy-start | bytes 3760132 | tf_op jit(solution)/shard_map/while
  60.3 2.2 %copy-start.1 = (f32[2,136,1152]{2,1,0:T(8,128)S(1)}, f32[2,136,1152]{2,1,0:T(8,128)}, u32[]{:S(2)}) copy-start(f32[2,136,1152]{2,1,0:T(8,128)} %get-tuple-element.698) | copy-start | bytes 3760132 | tf_op jit(solution)/shard_map/while
  60.3 2.5 %copy-start.3 = (f32[2,136,1152]{2,1,0:T(8,128)S(1)}, f32[2,136,1152]{2,1,0:T(8,128)}, u32[]{:S(2)}) copy-start(f32[2,136,1152]{2,1,0:T(8,128)} %get-tuple-element.699) | copy-start | bytes 3760132 | tf_op jit(solution)/shard_map/while
  73.7 2.2 %copy-start.1 = (f32[2,136,1152]{2,1,0:T(8,128)S(1)}, f32[2,136,1152]{2,1,0:T(8,128)}, u32[]{:S(2)}) copy-start(f32[2,136,1152]{2,1,0:T(8,128)} %get-tuple-element.698) | copy-start | bytes 3760132 | tf_op jit(solution)/shard_map/while
  73.8 2.5 %copy-start.3 = (f32[2,136,1152]{2,1,0:T(8,128)S(1)}, f32[2,136,1152]{2,1,0:T(8,128)}, u32[]{:S(2)}) copy-start(f32[2,136,1152]{2,1,0:T(8,128)} %get-tuple-element.699) | copy-start | bytes 3760132 | tf_op jit(solution)/shard_map/while
  87.2 2.2 %copy-start.1 = (f32[2,136,1152]{2,1,0:T(8,128)S(1)}, f32[2,136,1152]{2,1,0:T(8,128)}, u32[]{:S(2)}) copy-start(f32[2,136,1152]{2,1,0:T(8,128)} %get-tuple-element.698) | copy-start | bytes 3760132 | tf_op jit(solution)/shard_map/while
  87.2 2.5 %copy-start.3 = (f32[2,136,1152]{2,1,0:T(8,128)S(1)}, f32[2,136,1152]{2,1,0:T(8,128)}, u32[]{:S(2)}) copy-start(f32[2,136,1152]{2,1,0:T(8,128)} %get-tuple-element.699) | copy-start | bytes 3760132 | tf_op jit(solution)/shard_map/while
  100.6 2.2 %copy-start.1 = (f32[2,136,1152]{2,1,0:T(8,128)S(1)}, f32[2,136,1152]{2,1,0:T(8,128)}, u32[]{:S(2)}) copy-start(f32[2,136,1152]{2,1,0:T(8,128)} %get-tuple-element.698) | copy-start | bytes 3760132 | tf_op jit(solution)/shard_map/while
  100.7 2.5 %copy-start.3 = (f32[2,136,1152]{2,1,0:T(8,128)S(1)}, f32[2,136,1152]{2,1,0:T(8,128)}, u32[]{:S(2)}) copy-start(f32[2,136,1152]{2,1,0:T(8,128)} %get-tuple-element.699) | copy-start | bytes 3760132 | tf_op jit(solution)/shard_map/while
  114.1 2.2 %copy-start.1 = (f32[2,136,1152]{2,1,0:T(8,128)S(1)}, f32[2,136,1152]{2,1,0:T(8,128)}, u32[]{:S(2)}) copy-start(f32[2,136,1152]{2,1,0:T(8,128)} %get-tuple-element.698) | copy-start | bytes 3760132 | tf_op jit(solution)/shard_map/while
  114.1 2.5 %copy-start.3 = (f32[2,136,1152]{2,1,0:T(8,128)S(1)}, f32[2,136,1152]{2,1,0:T(8,128)}, u32[]{:S(2)}) copy-start(f32[2,136,1152]{2,1,0:T(8,128)} %get-tuple-element.699) | copy-start | bytes 3760132 | tf_op jit(solution)/shard_map/while
  127.6 2.2 %copy-start.1 = (f32[2,136,1152]{2,1,0:T(8,128)S(1)}, f32[2,136,1152]{2,1,0:T(8,128)}, u32[]{:S(2)}) copy-start(f32[2,136,1152]{2,1,0:T(8,128)} %get-tuple-element.698) | copy-start | bytes 3760132 | tf_op jit(solution)/shard_map/while
  127.6 2.5 %copy-start.3 = (f32[2,136,1152]{2,1,0:T(8,128)S(1)}, f32[2,136,1152]{2,1,0:T(8,128)}, u32[]{:S(2)}) copy-start(f32[2,136,1152]{2,1,0:T(8,128)} %get-tuple-element.699) | copy-start | bytes 3760132 | tf_op jit(solution)/shard_map/while
  141.0 2.2 %copy-start.1 = (f32[2,136,1152]{2,1,0:T(8,128)S(1)}, f32[2,136,1152]{2,1,0:T(8,128)}, u32[]{:S(2)}) copy-start(f32[2,136,1152]{2,1,0:T(8,128)} %get-tuple-element.698) | copy-start | bytes 3760132 | tf_op jit(solution)/shard_map/while
  141.0 2.5 %copy-start.3 = (f32[2,136,1152]{2,1,0:T(8,128)S(1)}, f32[2,136,1152]{2,1,0:T(8,128)}, u32[]{:S(2)}) copy-start(f32[2,136,1152]{2,1,0:T(8,128)} %get-tuple-element.699) | copy-start | bytes 3760132 | tf_op jit(solution)/shard_map/while
  (30 other events, 46.5 us)
where the time goes:
time: 212 us; the launch traced here: 211 us
  local copies, waits for them, and re-layouts  74.1 us (35%)
  blocking collectives  52.7 us (25%)
  other arithmetic  46.5 us (22%)
  loops' own time  16.9 us (8%)
  starting transfers between devices  11.2 us (5%)
  waiting for transfers between devices  4.81 us (2%)
  matrix products  4.33 us (2%)
    all_to_all x1, blocking collectives, shards(): lax.all_to_all(stencil, 'gx', split_axis=1, concat_axis=2, tiled=True)  52.7 us
    while x90, local copies, waits for them, and re-layouts  21.7 us
    another operation x1, loops' own time, shards(): lax.map(partial(probe_rows, prepared, local_rows), jnp.arange(9, dtype=jn...  16.9 us
    mul x9, other arithmetic, probe_rows(): vertical * fine_field  12.9 us
    broadcast_in_dim x9, local copies, waits for them, and re-layouts, shards(): lax.map(partial(probe_rows, prepared, local_rows), jnp.arange(9, dtype=jn...  11.4 us
    reshape x9, local copies, waits for them, and re-layouts, probe_rows(): kept = cols_done[2:2 + local_rows].reshape(local_rows // 2, 2, width)  10.5 us
    sub x9, other arithmetic, probe_rows(): centre * fine_field - east_face * jnp.roll(fine_field, -1, 1)  6.98 us
    dynamic_update_slice x9, local copies, waits for them, and re-layouts, shards(): lax.map(partial(probe_rows, prepared, local_rows), jnp.arange(9, dtype=jn...  6.72 us
  transfers between devices with their start and end apart: 4, of which 2 were waited for; matrix products, arithmetic and copies ran while one was open for 1% of the time, Pallas kernels for 0%

commit v1 on v0

--- a/solution.py
+++ b/solution.py
@@ -194,7 +194,10 @@
     )
     colours = colours.reshape(9, local_rows // 2, half_cols)
     stencil = by_offset(colours, row_start // 2, col_start // 2)
-    moved = lax.all_to_all(stencil, "gx", split_axis=1, concat_axis=2, tiled=True)
+    moved = jnp.concatenate(
+        lax.all_to_all(jnp.stack(jnp.split(stencil, lax.axis_size("gx"), axis=1)), "gx", 0, 0),
+        axis=2,
+    )
     return moved[:, None]
 
 

time: 212 us -> 196 us (0.925)
  blocking collectives: 52.7 us -> 33 us
  loops' own time: 16.9 us -> 20.1 us
    all_to_all x1, blocking collectives: 52.7 us -> 33 us  [shards(): lax.all_to_all(jnp.stack(jnp.split(stencil, lax.axis_size('gx'), axis=1))...]
    another operation x1, loops' own time: 16.9 us -> 20.1 us  [shards(): lax.map(partial(probe_rows, prepared, local_rows), jnp.arange(9, dtype=jn...]
where the time goes in v1:
time: 196 us; the launch traced here: 195 us
  local copies, waits for them, and re-layouts  74.2 us (38%)
  other arithmetic  46.7 us (24%)
  blocking collectives  33 us (17%)
  loops' own time  20.1 us (10%)
  starting transfers between devices  11.2 us (6%)
  waiting for transfers between devices  4.81 us (2%)
  matrix products  4.33 us (2%)
    all_to_all x1, blocking collectives, shards(): lax.all_to_all(jnp.stack(jnp.split(stencil, lax.axis_size('gx'), axis=1))...  33 us
    while x90, local copies, waits for them, and re-layouts  21.7 us
    another operation x1, loops' own time, shards(): lax.map(partial(probe_rows, prepared, local_rows), jnp.arange(9, dtype=jn...  20.1 us
    mul x9, other arithmetic, probe_rows(): vertical * fine_field  12.9 us
    broadcast_in_dim x9, local copies, waits for them, and re-layouts, shards(): lax.map(partial(probe_rows, prepared, local_rows), jnp.arange(9, dtype=jn...  11.4 us
    reshape x9, local copies, waits for them, and re-layouts, probe_rows(): kept = cols_done[2:2 + local_rows].reshape(local_rows // 2, 2, width)  10.5 us
    sub x9, other arithmetic, probe_rows(): centre * fine_field - east_face * jnp.roll(fine_field, -1, 1)  6.98 us
    dynamic_update_slice x9, local copies, waits for them, and re-layouts, shards(): lax.map(partial(probe_rows, prepared, local_rows), jnp.arange(9, dtype=jn...  6.71 us
  transfers between devices with their start and end apart: 4, of which 2 were waited for; matrix products, arithmetic and copies ran while one was open for 1% of the time, Pallas kernels for 0%

profile of v1, /device:TPU:4, one launch (start us, length us, event | category | flops | bytes accessed | tf_op | source)
XLA Modules:
  0.0 194.7 jit_solution(8240087640669405069)
XLA Ops:
  1.0 3.5 %collective-permute-start = (bf16[2,128,2]{2,1,0:T(8,128)(2,1)S(1)}, bf16[2,128,2]{2,1,0:T(8,128)(2,1)S(1)}, u32[]{:S(2)}, u32[]{:S(2)}) collective-permute-start(bf16[2,128,2]{2,1,0:T(8,128)(2,1)S(1)} %get-tuple-element.446), channel_id=1, source_target_pairs={{0,8},{8,16},{16,24},{1,9},{9,17},{17,25},{2,10},{10,18},{18,26},{... | collective-permute-start | bytes 3080 | tf_op jit(solution)/shard_map/ppermute | solution.py:16
  4.5 1.3 collective-permute-start.1
  7.1 3.5 %collective-permute-done.1 = bf16[2,128,2]{2,1,0:T(8,128)(2,1)S(1)} collective-permute-done((bf16[2,128,2]{2,1,0:T(8,128)(2,1)S(1)}, bf16[2,128,2]{2,1,0:T(8,128)(2,1)S(1)}, u32[]{:S(2)}, u32[]{:S(2)}) %collective-permute-start.1) | collective-permute-done | bytes 1056 | tf_op jit(solution)/shard_map/ppermute | solution.py:18
  11.3 1.9 collective-permute-start.2
  13.2 4.5 %collective-permute-start.3 = (bf16[2,2,1028]{2,1,0:T(2,128)(2,1)S(1)}, bf16[2,2,1028]{2,1,0:T(2,128)(2,1)S(1)}, u32[]{:S(2)}, u32[]{:S(2)}) collective-permute-start(bf16[2,2,1028]{2,1,0:T(2,128)(2,1)S(1)} %get-tuple-element.444), channel_id=1, source_target_pairs={{1,0},{2,1},{3,2},{4,3},{5,4},{6,5},{7,6},{9,8},{10,9},{11,10},{12... | collective-permute-start | bytes 24680 | tf_op jit(solution)/shard_map/ppermute | solution.py:18
  17.8 1.3 collective-permute-done.3
  21.1 4.2 %add_add_fusion = (f32[2,136,1152]{2,1,0:T(8,128)}, f32[2,136,1152]{2,1,0:T(8,128)S(1)}, f32[2,136,1152]{2,1,0:T(8,128)S(1)}, f32[2,136,1152]{2,1,0:T(8,128)S(1)}, f32[2,136,1152]{2,1,0:T(8,128)S(1)}) fusion(f32[136,1152]{1,0:T(8,128)S(1)} %divide_bitcast_fusion, pred[136,1152]{1,0:T(8,128)(4,1)S(1)} %broadcast_and_fusion, ...), kind=kLoop, calls=%fused_computation.66 | loop fusion | flops 13160448 | bytes 13233216 | tf_op jit(solution)/shard_map/add | solution.py:62
  27.6 125.0 %while.14 = (s32[]{:T(128)}, f32[9,64,1152]{2,1,0:T(8,128)}, s32[9]{0:T(128)S(1)}, f32[136,1152]{1,0:T(8,128)S(1)}, f32[136,1152]{1,0:T(8,128)S(1)}, /*index=5*/...) while((s32[]{:T(128)}, f32[9,64,1152]{2,1,0:T(8,128)}, ...), condition=%wide.region_1.2_spmd.clone.clone, body=%wide.region_0.1_spmd.clone.clone.sunk | while | flops 10339566 | bytes 78140304 | solution.py:184
  31.6 1.4 fusion.104
  39.5 1.3 slice_bitcast_fusion.6
  45.5 1.4 fusion.104
  53.4 1.3 slice_bitcast_fusion.6
  59.4 1.4 fusion.104
  73.3 1.4 fusion.104
  81.2 1.3 slice_bitcast_fusion.6
  87.2 1.4 fusion.104
  95.1 1.3 slice_bitcast_fusion.6
  101.0 1.4 fusion.104
  115.0 1.4 fusion.104
  128.8 1.4 fusion.104
  142.7 1.4 fusion.104
  152.6 4.3 %fusion.23 = f32[576,512]{1,0:T(8,128)S(1)} fusion(f32[576,1152]{1,0:T(8,128)} %bitcast.95, s32[512]{0:T(512)S(1)} %multiply_add_fusion), kind=kOutput, calls=%fused_computation.55 | convolution fusion | flops 4077453312 | bytes 3835904 | tf_op jit(solution)/shard_map/dot_general | solution.py:192
  159.1 33.0 %all_to_all.5 = f32[4,9,16,512]{3,2,1,0:T(8,128)S(1)} all-to-all(f32[4,9,16,512]{3,2,1,0:T(8,128)S(1)} %pad_maximum_fusion.10), channel_id=1, replica_groups=mesh['gx'=4,'gy'=8] {'gx'}, dimensions={0} | all-to-all | bytes 2359296 | tf_op jit(solution)/shard_map/all_to_all | solution.py:198
  192.9 1.8 broadcast_in_dim_reshape.3
  (434 shorter events, 96.9 us)
Async XLA Ops:
  1.0 6.1 %collective-permute-start = (bf16[2,128,2]{2,1,0:T(8,128)(2,1)S(1)}, bf16[2,128,2]{2,1,0:T(8,128)(2,1)S(1)}, u32[]{:S(2)}, u32[]{:S(2)}) collective-permute-start(bf16[2,128,2]{2,1,0:T(8,128)(2,1)S(1)} %get-tuple-element.446), channel_id=1, source_target_pairs={{0,8},{8,16},{16,24},{1,9},{9,17},{17,25},{2,10},{10,18},{18,26},{... | collective-permute-start | bytes 3080 | tf_op jit(solution)/shard_map/ppermute | solution.py:16
  4.5 6.2 %collective-permute-start.1 = (bf16[2,128,2]{2,1,0:T(8,128)(2,1)S(1)}, bf16[2,128,2]{2,1,0:T(8,128)(2,1)S(1)}, u32[]{:S(2)}, u32[]{:S(2)}) collective-permute-start(bf16[2,128,2]{2,1,0:T(8,128)(2,1)S(1)} %get-tuple-element.445), channel_id=1, source_target_pairs={{8,0},{16,8},{24,16},{9,1},{17,9},{25,17},{10,2},{18,10},{26,18},{... | collective-permute-start | bytes 3080 | tf_op jit(solution)/shard_map/ppermute | solution.py:18
  5.9 4.7 %copy-start.9 = (bf16[2,128,1024]{2,1,0:T(8,128)(2,1)S(1)}, bf16[2,128,1024]{2,1,0:T(8,128)(2,1)}, u32[]{:S(2)}) copy-start(bf16[2,128,1024]{2,1,0:T(8,128)(2,1)} %param.3) | copy-start | bytes 1572868
  11.3 6.5 %collective-permute-start.2 = (bf16[2,2,1028]{2,1,0:T(2,128)(2,1)S(1)}, bf16[2,2,1028]{2,1,0:T(2,128)(2,1)S(1)}, u32[]{:S(2)}, u32[]{:S(2)}) collective-permute-start(bf16[2,2,1028]{2,1,0:T(2,128)(2,1)S(1)} %get-tuple-element.443), channel_id=1, source_target_pairs={{0,1},{1,2},{2,3},{3,4},{4,5},{5,6},{6,7},{8,9},{9,10},{10,11},{11... | collective-permute-start | bytes 24680 | tf_op jit(solution)/shard_map/ppermute | solution.py:16
  13.2 5.9 %collective-permute-start.3 = (bf16[2,2,1028]{2,1,0:T(2,128)(2,1)S(1)}, bf16[2,2,1028]{2,1,0:T(2,128)(2,1)S(1)}, u32[]{:S(2)}, u32[]{:S(2)}) collective-permute-start(bf16[2,2,1028]{2,1,0:T(2,128)(2,1)S(1)} %get-tuple-element.444), channel_id=1, source_target_pairs={{1,0},{2,1},{3,2},{4,3},{5,4},{6,5},{7,6},{9,8},{10,9},{11,10},{12... | collective-permute-start | bytes 24680 | tf_op jit(solution)/shard_map/ppermute | solution.py:18
  25.3 2.3 %copy-start.6 = (f32[2,136,1152]{2,1,0:T(8,128)}, f32[2,136,1152]{2,1,0:T(8,128)S(1)}, u32[]{:S(2)}) copy-start(f32[2,136,1152]{2,1,0:T(8,128)S(1)} %get-tuple-element.651) | copy-start | bytes 3760132
  33.8 2.2 %copy-start.1 = (f32[2,136,1152]{2,1,0:T(8,128)S(1)}, f32[2,136,1152]{2,1,0:T(8,128)}, u32[]{:S(2)}) copy-start(f32[2,136,1152]{2,1,0:T(8,128)} %get-tuple-element.702) | copy-start | bytes 3760132 | tf_op jit(solution)/shard_map/while
  33.8 2.5 %copy-start.3 = (f32[2,136,1152]{2,1,0:T(8,128)S(1)}, f32[2,136,1152]{2,1,0:T(8,128)}, u32[]{:S(2)}) copy-start(f32[2,136,1152]{2,1,0:T(8,128)} %get-tuple-element.703) | copy-start | bytes 3760132 | tf_op jit(solution)/shard_map/while
  47.7 2.2 %copy-start.1 = (f32[2,136,1152]{2,1,0:T(8,128)S(1)}, f32[2,136,1152]{2,1,0:T(8,128)}, u32[]{:S(2)}) copy-start(f32[2,136,1152]{2,1,0:T(8,128)} %get-tuple-element.702) | copy-start | bytes 3760132 | tf_op jit(solution)/shard_map/while
  47.7 2.5 %copy-start.3 = (f32[2,136,1152]{2,1,0:T(8,128)S(1)}, f32[2,136,1152]{2,1,0:T(8,128)}, u32[]{:S(2)}) copy-start(f32[2,136,1152]{2,1,0:T(8,128)} %get-tuple-element.703) | copy-start | bytes 3760132 | tf_op jit(solution)/shard_map/while
  61.6 2.2 %copy-start.1 = (f32[2,136,1152]{2,1,0:T(8,128)S(1)}, f32[2,136,1152]{2,1,0:T(8,128)}, u32[]{:S(2)}) copy-start(f32[2,136,1152]{2,1,0:T(8,128)} %get-tuple-element.702) | copy-start | bytes 3760132 | tf_op jit(solution)/shard_map/while
  61.6 2.5 %copy-start.3 = (f32[2,136,1152]{2,1,0:T(8,128)S(1)}, f32[2,136,1152]{2,1,0:T(8,128)}, u32[]{:S(2)}) copy-start(f32[2,136,1152]{2,1,0:T(8,128)} %get-tuple-element.703) | copy-start | bytes 3760132 | tf_op jit(solution)/shard_map/while
  75.5 2.2 %copy-start.1 = (f32[2,136,1152]{2,1,0:T(8,128)S(1)}, f32[2,136,1152]{2,1,0:T(8,128)}, u32[]{:S(2)}) copy-start(f32[2,136,1152]{2,1,0:T(8,128)} %get-tuple-element.702) | copy-start | bytes 3760132 | tf_op jit(solution)/shard_map/while
  75.5 2.5 %copy-start.3 = (f32[2,136,1152]{2,1,0:T(8,128)S(1)}, f32[2,136,1152]{2,1,0:T(8,128)}, u32[]{:S(2)}) copy-start(f32[2,136,1152]{2,1,0:T(8,128)} %get-tuple-element.703) | copy-start | bytes 3760132 | tf_op jit(solution)/shard_map/while
  89.4 2.2 %copy-start.1 = (f32[2,136,1152]{2,1,0:T(8,128)S(1)}, f32[2,136,1152]{2,1,0:T(8,128)}, u32[]{:S(2)}) copy-start(f32[2,136,1152]{2,1,0:T(8,128)} %get-tuple-element.702) | copy-start | bytes 3760132 | tf_op jit(solution)/shard_map/while
  89.4 2.5 %copy-start.3 = (f32[2,136,1152]{2,1,0:T(8,128)S(1)}, f32[2,136,1152]{2,1,0:T(8,128)}, u32[]{:S(2)}) copy-start(f32[2,136,1152]{2,1,0:T(8,128)} %get-tuple-element.703) | copy-start | bytes 3760132 | tf_op jit(solution)/shard_map/while
  103.3 2.2 %copy-start.1 = (f32[2,136,1152]{2,1,0:T(8,128)S(1)}, f32[2,136,1152]{2,1,0:T(8,128)}, u32[]{:S(2)}) copy-start(f32[2,136,1152]{2,1,0:T(8,128)} %get-tuple-element.702) | copy-start | bytes 3760132 | tf_op jit(solution)/shard_map/while
  103.3 2.5 %copy-start.3 = (f32[2,136,1152]{2,1,0:T(8,128)S(1)}, f32[2,136,1152]{2,1,0:T(8,128)}, u32[]{:S(2)}) copy-start(f32[2,136,1152]{2,1,0:T(8,128)} %get-tuple-element.703) | copy-start | bytes 3760132 | tf_op jit(solution)/shard_map/while
  117.2 2.2 %copy-start.1 = (f32[2,136,1152]{2,1,0:T(8,128)S(1)}, f32[2,136,1152]{2,1,0:T(8,128)}, u32[]{:S(2)}) copy-start(f32[2,136,1152]{2,1,0:T(8,128)} %get-tuple-element.702) | copy-start | bytes 3760132 | tf_op jit(solution)/shard_map/while
  117.2 2.5 %copy-start.3 = (f32[2,136,1152]{2,1,0:T(8,128)S(1)}, f32[2,136,1152]{2,1,0:T(8,128)}, u32[]{:S(2)}) copy-start(f32[2,136,1152]{2,1,0:T(8,128)} %get-tuple-element.703) | copy-start | bytes 3760132 | tf_op jit(solution)/shard_map/while
  131.1 2.2 %copy-start.1 = (f32[2,136,1152]{2,1,0:T(8,128)S(1)}, f32[2,136,1152]{2,1,0:T(8,128)}, u32[]{:S(2)}) copy-start(f32[2,136,1152]{2,1,0:T(8,128)} %get-tuple-element.702) | copy-start | bytes 3760132 | tf_op jit(solution)/shard_map/while
  131.1 2.5 %copy-start.3 = (f32[2,136,1152]{2,1,0:T(8,128)S(1)}, f32[2,136,1152]{2,1,0:T(8,128)}, u32[]{:S(2)}) copy-start(f32[2,136,1152]{2,1,0:T(8,128)} %get-tuple-element.703) | copy-start | bytes 3760132 | tf_op jit(solution)/shard_map/while
  145.0 2.2 %copy-start.1 = (f32[2,136,1152]{2,1,0:T(8,128)S(1)}, f32[2,136,1152]{2,1,0:T(8,128)}, u32[]{:S(2)}) copy-start(f32[2,136,1152]{2,1,0:T(8,128)} %get-tuple-element.702) | copy-start | bytes 3760132 | tf_op jit(solution)/shard_map/while
  145.0 2.5 %copy-start.3 = (f32[2,136,1152]{2,1,0:T(8,128)S(1)}, f32[2,136,1152]{2,1,0:T(8,128)}, u32[]{:S(2)}) copy-start(f32[2,136,1152]{2,1,0:T(8,128)} %get-tuple-element.703) | copy-start | bytes 3760132 | tf_op jit(solution)/shard_map/while
  (30 other events, 46.5 us)
